TPU v7x, 32 devices: a whole 2x2x4 slice. The times are simulated.
32 devices in a mesh: src: 4 (over z), delay: 8 (over y, x, core).
Axes of the slice: x: 2, y: 2, z: 4, core: 2. Of those that a mesh axis runs over, the one named last changes fastest.
Arguments:
- history: float32 [32, 16, 16, 128], P('delay', 'src'), may hold values from -6 to 6
- slot_map: int32 [32], P('delay'), may hold values from 0 to 3, as said below
- interaction: float32 [1536, 128, 128], P(('src', 'delay')), may hold values from -0.0546875 to 0.0546875
- pattern: int32 [3, 1536], P(None, ('src', 'delay')), may hold values from 0 to 15, as said below
- live: int32 [32], P(('src', 'delay')), may hold values from 12 to 48
- near_inverse: float32 [16, 128, 128], P('src'), may hold values from -0.5 to 0.5
- incident: float32 [4, 16, 16, 128], P(None, 'src'), may hold values from -6 to 6
Outputs:
- currents: float32 [4, 16, 16, 128], P(None, 'src')
Inputs may be any that keep to these rules, and one draw needn't show every extreme that they name: `slot_map`: each band's 4 entries are a cyclic rotation of 0 .. 3. `pattern`: row 0 lies in 0 .. 3, row 1 in 0 .. 15, row 2 in 0 .. 3.
All inputs are finite; a program needn't handle non-finite values.
Results may differ from a plain program's by a relative error of at most 0.0003.
Values sent between devices are 32-bit elements; how exact they have to be, the bound alone decides.
No kernel may reach another device: no remote copies, remote signals or barrier semaphores. Data moves between devices by JAX's collectives and lax.ppermute only.
A program may use at most 64 MiB of HBM per device.

v0:
```python
import jax
import jax.numpy as jnp
from jax import lax
from jax.sharding import PartitionSpec as P


def shifted(x, axis, by):
    devices = lax.axis_size(axis)
    pairs = [(i, i + by) for i in range(devices) if 0 <= i + by < devices]
    return lax.ppermute(x, axis, pairs)


def slot_holding(slot_map, wanted, moment):
    length = slot_map.shape[0]
    positions = jnp.arange(length, dtype=jnp.int32)
    return jnp.sum(jnp.where((slot_map + moment) % length == wanted, positions, 0))


def body(history, slot_map, interaction, pattern, live, near_inverse, incident):
    slot_count = history.shape[0]
    group_blocks = history.shape[1]
    columns = history.shape[2]
    block_width = history.shape[3]
    moments = incident.shape[0]
    pair_count = interaction.shape[0]
    positions = jnp.arange(slot_count, dtype=jnp.int32)
    at_front = lax.axis_index("delay") == 0
    in_use = (jnp.arange(pair_count, dtype=jnp.int32) < live[0]).astype(jnp.float32)
    row_match = pattern[0][None, :] == jnp.arange(group_blocks, dtype=jnp.int32)[:, None]
    selector = row_match.astype(jnp.float32) * in_use[None, :]
    band_state = lax.all_gather(history, "src", axis=1, tiled=True)
    results = []
    newest = None
    for moment in range(moments):
        if moment > 0:
            vacated = slot_holding(slot_map, slot_count - 1, moment - 1)
            outgoing_slot = lax.dynamic_index_in_dim(band_state, vacated, 0, keepdims=False)
            incoming = shifted(outgoing_slot, "delay", 1)
            entering = jnp.where(at_front, newest, incoming)
            band_state = lax.dynamic_update_index_in_dim(band_state, entering, vacated, 0)
        holder_match = (slot_map[None, :] + moment) % slot_count == pattern[2][:, None]
        holder = jnp.sum(jnp.where(holder_match, positions[None, :], 0), axis=1)
        picked = band_state[holder, pattern[1]]
        products = jnp.einsum("pab,prb->pra", interaction, picked, precision=lax.Precision.HIGHEST)
        partial_field = jnp.dot(
            selector,
            products.reshape(pair_count, columns * block_width),
            precision=lax.Precision.HIGHEST,
        )
        partial_field = partial_field.reshape(group_blocks, columns, block_width)
        field_sum = lax.psum(partial_field, "delay")
        current = jnp.einsum(
            "iab,irb->ira",
            near_inverse,
            incident[moment] - field_sum,
            precision=lax.Precision.HIGHEST,
        )
        results.append(current)
        if moment + 1 < moments:
            newest = lax.all_gather(current, "src", axis=0, tiled=True)
    return jnp.stack(results)


def solution(mesh):
    return jax.shard_map(
        body,
        mesh=mesh,
        in_specs=(
            P("delay", "src", None, None),
            P("delay"),
            P(("src", "delay"), None, None),
            P(None, ("src", "delay")),
            P(("src", "delay")),
            P("src", None, None),
            P(None, "src", None, None),
        ),
        out_specs=P(None, "src", None, None),
        check_vma=False,
    )
```

profile of v0, /device:TPU:4, one launch (start us, length us, event | category | flops | bytes accessed | tf_op | source)
XLA Modules:
  0.0 216.7 jit_solution(3523601571943106550)
XLA Ops:
  0.0 1.5 fusion.45
  1.5 18.1 %all_gather.12 = f32[4,16,16,128]{3,2,1,0:T(8,128)} all-gather(f32[4,4,16,128]{3,2,1,0:T(8,128)} %param.7), channel_id=1, replica_groups=mesh['src'=4,'delay'=8] {'src'}, dimensions={1}, use_global_device_ids=true | all-gather | bytes 655360 | tf_op jit(solution)/shard_map/all_gather | solution.py:31
  21.5 1.6 dynamic-slice_bitcast_fusion.2
  23.1 1.9 collective-permute-start
  25.0 0.8 slice_bitcast_fusion.1
  25.9 0.7 fusion.64
  26.6 2.6 %gather_fusion = f32[48,16,128]{2,1,0:T(8,128)} fusion(f32[4,16,16,128]{3,2,1,0:T(8,128)} %all_gather.12, s32[48]{0:T(128)S(1)} %get-tuple-element.25), kind=kCustom, calls=%fused_computation | custom fusion | bytes 786816 | tf_op jit(solution)/shard_map/gather | solution.py:43
  29.9 6.0 %fusion.74 = f32[48,16,128]{2,1,0:T(8,128)S(1)} fusion(f32[48,16,128]{2,1,0:T(8,128)} %gather_fusion, f32[48,128,128]{2,1,0:T(8,128)S(1)} %copy-done), kind=kOutput, calls=%fused_computation.121 | convolution fusion | flops 150994944 | bytes 3932160 | tf_op jit(solution)/shard_map/pab,prb->pra/dot_general | solution.py:44
  36.3 24.8 %psum.28 = f32[4,16,128]{2,0,1:T(4,128)S(1)} all-reduce(f32[4,16,128]{2,0,1:T(4,128)S(1)} %fusion.9), channel_id=1, replica_groups=mesh['src'=4,'delay'=8] {'delay'}, use_global_device_ids=true, to_apply=%region_1.2 | all-reduce | flops 8192 | bytes 65536 | tf_op jit(solution)/shard_map/psum | solution.py:51
  61.1 1.4 fusion.73
  66.7 13.4 %all_gather.13 = f32[16,16,128]{2,1,0:T(8,128)S(1)} all-gather(f32[4,16,128]{2,1,0:T(8,128)S(1)} %fusion.21), channel_id=1, replica_groups=mesh['src'=4,'delay'=8] {'src'}, dimensions={0}, use_global_device_ids=true | all-gather | bytes 163840 | tf_op jit(solution)/shard_map/all_gather | solution.py:60
  80.0 1.6 bitcast_dynamic-update-slice_fusion.2
  81.6 2.6 %gather_fusion.1 = f32[48,16,128]{2,1,0:T(8,128)} fusion(f32[4,16,16,128]{3,2,1,0:T(8,128)} %bitcast_dynamic-update-slice_fusion.2, s32[48]{0:T(128)S(1)} %get-tuple-element.24), kind=kCustom, calls=%fused_computation.1 | custom fusion | bytes 786816 | tf_op jit(solution)/shard_map/gather | solution.py:43
  84.3 6.0 %fusion.75 = f32[48,16,128]{2,1,0:T(8,128)S(1)} fusion(f32[48,16,128]{2,1,0:T(8,128)} %gather_fusion.1, f32[48,128,128]{2,1,0:T(8,128)S(1)} %copy-done), kind=kOutput, calls=%fused_computation.122 | convolution fusion | flops 150994944 | bytes 3932160 | tf_op jit(solution)/shard_map/pab,prb->pra/dot_general | solution.py:44
  90.2 1.0 fusion.6
  91.3 22.9 %psum.29 = f32[4,16,128]{2,0,1:T(4,128)S(1)} all-reduce(f32[4,16,128]{2,0,1:T(4,128)} %fusion.6), channel_id=1, replica_groups=mesh['src'=4,'delay'=8] {'delay'}, use_global_device_ids=true, to_apply=%region_4.5 | all-reduce | flops 8192 | bytes 65536 | tf_op jit(solution)/shard_map/psum | solution.py:51
  114.2 0.9 dynamic-slice_bitcast_fusion.1
  115.1 1.9 collective-permute-start.1
  117.6 13.9 %all_gather.14 = f32[16,16,128]{2,1,0:T(8,128)S(1)} all-gather(f32[4,16,128]{2,1,0:T(8,128)S(1)} %fusion.19), channel_id=1, replica_groups=mesh['src'=4,'delay'=8] {'src'}, dimensions={0}, use_global_device_ids=true | all-gather | bytes 163840 | tf_op jit(solution)/shard_map/all_gather | solution.py:60
  132.1 2.6 %gather_fusion.2 = f32[48,16,128]{2,1,0:T(8,128)} fusion(f32[4,16,16,128]{3,2,1,0:T(8,128)} %bitcast_dynamic-update-slice_fusion.1, s32[48]{0:T(128)S(1)} %get-tuple-element.23), kind=kCustom, calls=%fused_computation.2 | custom fusion | bytes 786816 | tf_op jit(solution)/shard_map/gather | solution.py:43
  134.7 6.0 %fusion.76 = f32[48,16,128]{2,1,0:T(8,128)S(1)} fusion(f32[48,16,128]{2,1,0:T(8,128)} %gather_fusion.2, f32[48,128,128]{2,1,0:T(8,128)S(1)} %copy-done), kind=kOutput, calls=%fused_computation.123 | convolution fusion | flops 150994944 | bytes 3932160 | tf_op jit(solution)/shard_map/pab,prb->pra/dot_general | solution.py:44
  140.7 1.0 fusion.3
  141.7 22.9 %psum.30 = f32[4,16,128]{2,0,1:T(4,128)S(1)} all-reduce(f32[4,16,128]{2,0,1:T(4,128)} %fusion.3), channel_id=1, replica_groups=mesh['src'=4,'delay'=8] {'delay'}, use_global_device_ids=true, to_apply=%region_7.8 | all-reduce | flops 8192 | bytes 65536 | tf_op jit(solution)/shard_map/psum | solution.py:51
  164.6 0.9 dynamic-slice_bitcast_fusion
  165.6 1.9 collective-permute-start.2
  168.0 13.5 %all_gather.15 = f32[16,16,128]{2,1,0:T(8,128)S(1)} all-gather(f32[4,16,128]{2,1,0:T(8,128)S(1)} %fusion.17), channel_id=1, replica_groups=mesh['src'=4,'delay'=8] {'src'}, dimensions={0}, use_global_device_ids=true | all-gather | bytes 163840 | tf_op jit(solution)/shard_map/all_gather | solution.py:60
  182.2 2.6 %gather_fusion.3 = f32[48,16,128]{2,1,0:T(8,128)} fusion(f32[4,16,16,128]{3,2,1,0:T(8,128)} %bitcast_dynamic-update-slice_fusion, s32[48]{0:T(128)S(1)} %get-tuple-element.9), kind=kCustom, calls=%fused_computation.3 | custom fusion | bytes 786816 | tf_op jit(solution)/shard_map/gather | solution.py:43
  184.9 6.0 %fusion.77 = f32[48,16,128]{2,1,0:T(8,128)S(1)} fusion(f32[48,16,128]{2,1,0:T(8,128)} %gather_fusion.3, f32[48,128,128]{2,1,0:T(8,128)S(1)} %copy-done), kind=kOutput, calls=%fused_computation.124 | convolution fusion | flops 150994944 | bytes 3932160 | tf_op jit(solution)/shard_map/pab,prb->pra/dot_general | solution.py:44
  190.8 1.0 fusion
  191.9 22.9 %psum.31 = f32[4,16,128]{2,0,1:T(4,128)S(1)} all-reduce(f32[4,16,128]{2,0,1:T(4,128)} %fusion), channel_id=1, replica_groups=mesh['src'=4,'delay'=8] {'delay'}, use_global_device_ids=true, to_apply=%region_10.11 | all-reduce | flops 8192 | bytes 65536 | tf_op jit(solution)/shard_map/psum | solution.py:51
  214.8 0.8 fusion.12
  216.0 0.7 pad_maximum_fusion
  (26 shorter events, 3.9 us)
Async XLA Ops:
  0.0 29.9 %copy-start = (f32[48,128,128]{2,1,0:T(8,128)S(1)}, f32[48,128,128]{2,1,0:T(8,128)}, u32[]{:S(2)}) copy-start(f32[48,128,128]{2,1,0:T(8,128)} %param.9) | copy-start | bytes 9437188
  1.5 61.0 %copy-start.1 = (f32[4,128,128]{2,1,0:T(8,128)S(1)}, f32[4,128,128]{2,1,0:T(8,128)}, u32[]{:S(2)}) copy-start(f32[4,128,128]{2,1,0:T(8,128)} %param.12) | copy-start | bytes 786436
  23.1 56.9 %collective-permute-start = (f32[16,16,128]{2,1,0:T(8,128)}, f32[16,16,128]{2,1,0:T(8,128)}, u32[]{:S(2)}, u32[]{:S(2)}) collective-permute-start(f32[16,16,128]{2,1,0:T(8,128)} %dynamic-slice_bitcast_fusion.2), channel_id=1, source_target_pairs={{0,1},{1,2},{2,3},{3,4},{4,5},{5,6},{6,7},{8,9},{9,10},{10,11},{11... | collective-permute-start | bytes 393224 | tf_op jit(solution)/shard_map/ppermute | solution.py:10
  29.9 6.0 %copy-start.2 = (f32[48]{0:T(128)}, f32[48]{0:T(128)S(1)}, u32[]{:S(2)}) copy-start(f32[48]{0:T(128)S(1)} %compare_convert_fusion) | copy-start | bytes 580
  62.5 27.7 %copy-start.3 = (f32[48]{0:T(128)S(1)}, f32[48]{0:T(128)}, u32[]{:S(2)}) copy-start(f32[48]{0:T(128)} %copy-done.2) | copy-start | bytes 580
  90.2 50.5 %copy-start.4 = (f32[48]{0:T(128)S(1)}, f32[48]{0:T(128)}, u32[]{:S(2)}) copy-start(f32[48]{0:T(128)} %copy-done.2) | copy-start | bytes 580
  115.1 16.3 %collective-permute-start.1 = (f32[16,16,128]{2,1,0:T(8,128)S(1)}, f32[16,16,128]{2,1,0:T(8,128)S(1)}, u32[]{:S(2)}, u32[]{:S(2)}) collective-permute-start(f32[16,16,128]{2,1,0:T(8,128)S(1)} %dynamic-slice_bitcast_fusion.1), channel_id=1, source_target_pairs={{0,1},{1,2},{2,3},{3,4},{4,5},{5,6},{6,7},{8,9},{9,10},{10,11},{11... | collective-permute-start | bytes 393224 | tf_op jit(solution)/shard_map/ppermute | solution.py:10
  165.6 16.0 %collective-permute-start.2 = (f32[16,16,128]{2,1,0:T(8,128)S(1)}, f32[16,16,128]{2,1,0:T(8,128)S(1)}, u32[]{:S(2)}, u32[]{:S(2)}) collective-permute-start(f32[16,16,128]{2,1,0:T(8,128)S(1)} %dynamic-slice_bitcast_fusion), channel_id=1, source_target_pairs={{0,1},{1,2},{2,3},{3,4},{4,5},{5,6},{6,7},{8,9},{9,10},{10,11},{11... | collective-permute-start | bytes 393224 | tf_op jit(solution)/shard_map/ppermute | solution.py:10
where the time goes:
time: 218 us; the launch traced here: 217 us
  blocking collectives  152 us (70%)
  matrix products  29.4 us (13%)
  local copies, waits for them, and re-layouts  16.2 us (7%)
  other arithmetic  6.73 us (3%)
  between operations  6.34 us (3%)
  starting transfers between devices  5.75 us (3%)
    psum x4, blocking collectives, body(): field_sum = lax.psum(partial_field, 'delay')  93.5 us
    all_gather x3, blocking collectives, body(): newest = lax.all_gather(current, 'src', axis=0, tiled=True)  40.7 us
    dot_general x4, matrix products, body(): jnp.einsum('pab,prb->pra', interaction, picked, precision=lax.Precision.H...  23.8 us
    all_gather x1, blocking collectives, body(): band_state = lax.all_gather(history, 'src', axis=1, tiled=True)  18.1 us
    gather x4, local copies, waits for them, and re-layouts, body(): picked = band_state[holder, pattern[1]]  10.6 us
    ppermute x3, starting transfers between devices, shifted(): return lax.ppermute(x, axis, pairs)  5.75 us
  transfers between devices with their start and end apart: 3, of which 0 were waited for; matrix products, arithmetic and copies ran while one was open for 6% of the time, Pallas kernels for 0%

commit v1 on v0

--- a/solution.py
+++ b/solution.py
@@ -2,6 +2,19 @@
 import jax.numpy as jnp
 from jax import lax
 from jax.sharding import PartitionSpec as P
+
+
+def gather_around(x, axis, dim):
+    ways = lax.axis_size(axis)
+    up = [(d, (d + 1) % ways) for d in range(ways)]
+    down = [(d, (d - 1) % ways) for d in range(ways)]
+    earlier, later = ([x], [x])
+    for _ in range(ways // 2):
+        earlier.append(lax.ppermute(earlier[-1], axis, up))
+    for _ in range((ways - 1) // 2):
+        later.append(lax.ppermute(later[-1], axis, down))
+    line = jnp.concatenate([*earlier[::-1], *later[1:]], axis=dim)
+    return jnp.roll(line, (lax.axis_index(axis) - ways // 2) * x.shape[dim], axis=dim)
 
 
 def shifted(x, axis, by):
@@ -28,7 +41,7 @@
     in_use = (jnp.arange(pair_count, dtype=jnp.int32) < live[0]).astype(jnp.float32)
     row_match = pattern[0][None, :] == jnp.arange(group_blocks, dtype=jnp.int32)[:, None]
     selector = row_match.astype(jnp.float32) * in_use[None, :]
-    band_state = lax.all_gather(history, "src", axis=1, tiled=True)
+    band_state = gather_around(history, "src", 1)
     results = []
     newest = None
     for moment in range(moments):

time: 218 us -> 205 us (0.940)
  blocking collectives: 152 us -> 132 us
  starting transfers between devices: 5.75 us -> 9.64 us
  local copies, waits for them, and re-layouts: 16.2 us -> 19.7 us
    all_gather x1 -> x0, blocking collectives: 18.1 us -> none  [body(): band_state = lax.all_gather(history, 'src', axis=1, tiled=True)]
    ppermute x0 -> x3, starting transfers between devices: none -> 3.88 us  [the longest x1 2.25 us: gather_around(): later.append(lax.ppermute(later[-1], axis, down))]
    unnamed x10 -> x25, local copies, waits for them, and re-layouts: 0.02 us -> 2.9 us
    psum x4, blocking collectives: 93.5 us -> 90.8 us  [body(): field_sum = lax.psum(partial_field, 'delay')]
  transfers between devices with their start and end apart: 3 -> 6, of which waited for: 0 -> 0; matrix products, arithmetic and copies ran while one was open for 6% -> 4% of each run, Pallas kernels for 0% -> 0%
where the time goes in v1:
time: 205 us; the launch traced here: 204 us
  blocking collectives  132 us (64%)
  matrix products  29.5 us (14%)
  local copies, waits for them, and re-layouts  19.7 us (10%)
  starting transfers between devices  9.64 us (5%)
  between operations  6.72 us (3%)
  other arithmetic  6.28 us (3%)
    psum x4, blocking collectives, body(): field_sum = lax.psum(partial_field, 'delay')  90.8 us
    all_gather x3, blocking collectives, body(): newest = lax.all_gather(current, 'src', axis=0, tiled=True)  41.3 us
    dot_general x4, matrix products, body(): jnp.einsum('pab,prb->pra', interaction, picked, precision=lax.Precision.H...  23.8 us
    gather x4, local copies, waits for them, and re-layouts, body(): picked = band_state[holder, pattern[1]]  10.5 us
    ppermute x3, starting transfers between devices, shifted(): return lax.ppermute(x, axis, pairs)  5.76 us
  transfers between devices with their start and end apart: 6, of which 0 were waited for; matrix products, arithmetic and copies ran while one was open for 4% of the time, Pallas kernels for 0%

profile of v1, /device:TPU:4, one launch (start us, length us, event | category | flops | bytes accessed | tf_op | source)
XLA Modules:
  0.0 203.9 jit_solution(16368991288670428130)
XLA Ops:
  0.0 1.6 collective-permute-start
  1.6 2.2 %collective-permute-start.2 = (f32[4,4,16,128]{3,2,1,0:T(8,128)}, f32[4,4,16,128]{3,2,1,0:T(8,128)S(1)}, u32[]{:S(2)}, u32[]{:S(2)}) collective-permute-start(f32[4,4,16,128]{3,2,1,0:T(8,128)} %param.7), channel_id=1, source_target_pairs={{0,24},{8,0},{16,8},{24,16},{1,25},{9,1},{17,9},{25,17},{2,26},{10... | collective-permute-start | bytes 393224 | tf_op jit(solution)/shard_map/ppermute | solution.py:15
  3.8 1.4 fusion.45
  5.2 1.3 slice_bitcast_fusion.1
  6.5 1.4 fusion.73
  15.9 0.9 constant_dynamic-update-slice_fusion.5
  16.9 0.9 constant_dynamic-update-slice_fusion.1
  17.9 1.0 copy-done.2
  19.7 2.6 %gather_fusion = f32[48,16,128]{2,1,0:T(8,128)} fusion(f32[4,16,16,128]{3,2,1,0:T(8,128)} %constant_dynamic-slice_fusion, s32[48]{0:T(128)S(1)} %get-tuple-element.25), kind=kCustom, calls=%fused_computation | custom fusion | bytes 786816 | tf_op jit(solution)/shard_map/gather | solution.py:56
  22.3 6.0 %fusion.74 = f32[48,16,128]{2,1,0:T(8,128)S(1)} fusion(f32[48,16,128]{2,1,0:T(8,128)} %gather_fusion, f32[48,128,128]{2,1,0:T(8,128)S(1)} %copy-done), kind=kOutput, calls=%fused_computation.130 | convolution fusion | flops 150994944 | bytes 3932160 | tf_op jit(solution)/shard_map/pab,prb->pra/dot_general | solution.py:57
  28.7 22.6 %psum.28 = f32[4,16,128]{2,0,1:T(4,128)S(1)} all-reduce(f32[4,16,128]{2,0,1:T(4,128)S(1)} %fusion.9), channel_id=1, replica_groups=mesh['src'=4,'delay'=8] {'delay'}, use_global_device_ids=true, to_apply=%region_1.2 | all-reduce | flops 8192 | bytes 65536 | tf_op jit(solution)/shard_map/psum | solution.py:64
  51.3 0.9 dynamic-slice_bitcast_fusion.2
  52.2 1.9 collective-permute-start.3
  54.7 14.4 %all_gather.9 = f32[16,16,128]{2,1,0:T(8,128)S(1)} all-gather(f32[4,16,128]{2,1,0:T(8,128)S(1)} %fusion.21), channel_id=1, replica_groups=mesh['src'=4,'delay'=8] {'src'}, dimensions={0}, use_global_device_ids=true | all-gather | bytes 163840 | tf_op jit(solution)/shard_map/all_gather | solution.py:73
  69.8 2.6 %gather_fusion.1 = f32[48,16,128]{2,1,0:T(8,128)} fusion(f32[4,16,16,128]{3,2,1,0:T(8,128)} %bitcast_dynamic-update-slice_fusion.2, s32[48]{0:T(128)S(1)} %get-tuple-element.24), kind=kCustom, calls=%fused_computation.1 | custom fusion | bytes 786816 | tf_op jit(solution)/shard_map/gather | solution.py:56
  72.4 6.0 %fusion.75 = f32[48,16,128]{2,1,0:T(8,128)S(1)} fusion(f32[48,16,128]{2,1,0:T(8,128)} %gather_fusion.1, f32[48,128,128]{2,1,0:T(8,128)S(1)} %copy-done), kind=kOutput, calls=%fused_computation.131 | convolution fusion | flops 150994944 | bytes 3932160 | tf_op jit(solution)/shard_map/pab,prb->pra/dot_general | solution.py:57
  78.3 1.2 fusion.6
  79.5 22.3 %psum.29 = f32[4,16,128]{2,0,1:T(4,128)S(1)} all-reduce(f32[4,16,128]{2,0,1:T(4,128)S(1)} %fusion.6), channel_id=1, replica_groups=mesh['src'=4,'delay'=8] {'delay'}, use_global_device_ids=true, to_apply=%region_4.5 | all-reduce | flops 8192 | bytes 65536 | tf_op jit(solution)/shard_map/psum | solution.py:64
  101.9 0.9 dynamic-slice_bitcast_fusion.1
  102.8 1.9 collective-permute-start.4
  105.3 13.5 %all_gather.10 = f32[16,16,128]{2,1,0:T(8,128)S(1)} all-gather(f32[4,16,128]{2,1,0:T(8,128)S(1)} %fusion.19), channel_id=1, replica_groups=mesh['src'=4,'delay'=8] {'src'}, dimensions={0}, use_global_device_ids=true | all-gather | bytes 163840 | tf_op jit(solution)/shard_map/all_gather | solution.py:73
  119.5 2.6 %gather_fusion.2 = f32[48,16,128]{2,1,0:T(8,128)} fusion(f32[4,16,16,128]{3,2,1,0:T(8,128)} %bitcast_dynamic-update-slice_fusion.1, s32[48]{0:T(128)S(1)} %get-tuple-element.23), kind=kCustom, calls=%fused_computation.2 | custom fusion | bytes 786816 | tf_op jit(solution)/shard_map/gather | solution.py:56
  122.1 6.0 %fusion.76 = f32[48,16,128]{2,1,0:T(8,128)S(1)} fusion(f32[48,16,128]{2,1,0:T(8,128)} %gather_fusion.2, f32[48,128,128]{2,1,0:T(8,128)S(1)} %copy-done), kind=kOutput, calls=%fused_computation.132 | convolution fusion | flops 150994944 | bytes 3932160 | tf_op jit(solution)/shard_map/pab,prb->pra/dot_general | solution.py:57
  128.1 1.0 fusion.3
  129.1 22.9 %psum.30 = f32[4,16,128]{2,0,1:T(4,128)S(1)} all-reduce(f32[4,16,128]{2,0,1:T(4,128)} %fusion.3), channel_id=1, replica_groups=mesh['src'=4,'delay'=8] {'delay'}, use_global_device_ids=true, to_apply=%region_7.8 | all-reduce | flops 8192 | bytes 65536 | tf_op jit(solution)/shard_map/psum | solution.py:64
  152.0 0.9 dynamic-slice_bitcast_fusion
  152.9 1.9 collective-permute-start.5
  155.4 13.4 %all_gather.11 = f32[16,16,128]{2,1,0:T(8,128)S(1)} all-gather(f32[4,16,128]{2,1,0:T(8,128)S(1)} %fusion.17), channel_id=1, replica_groups=mesh['src'=4,'delay'=8] {'src'}, dimensions={0}, use_global_device_ids=true | all-gather | bytes 163840 | tf_op jit(solution)/shard_map/all_gather | solution.py:73
  169.4 2.6 %gather_fusion.3 = f32[48,16,128]{2,1,0:T(8,128)} fusion(f32[4,16,16,128]{3,2,1,0:T(8,128)} %bitcast_dynamic-update-slice_fusion, s32[48]{0:T(128)S(1)} %get-tuple-element.9), kind=kCustom, calls=%fused_computation.3 | custom fusion | bytes 786816 | tf_op jit(solution)/shard_map/gather | solution.py:56
  172.0 6.0 %fusion.77 = f32[48,16,128]{2,1,0:T(8,128)S(1)} fusion(f32[48,16,128]{2,1,0:T(8,128)} %gather_fusion.3, f32[48,128,128]{2,1,0:T(8,128)S(1)} %copy-done), kind=kOutput, calls=%fused_computation.133 | convolution fusion | flops 150994944 | bytes 3932160 | tf_op jit(solution)/shard_map/pab,prb->pra/dot_general | solution.py:57
  178.0 1.0 fusion
  179.0 22.9 %psum.31 = f32[4,16,128]{2,0,1:T(4,128)S(1)} all-reduce(f32[4,16,128]{2,0,1:T(4,128)} %fusion), channel_id=1, replica_groups=mesh['src'=4,'delay'=8] {'delay'}, use_global_device_ids=true, to_apply=%region_10.11 | all-reduce | flops 8192 | bytes 65536 | tf_op jit(solution)/shard_map/psum | solution.py:64
  (48 shorter events, 8.4 us)
Async XLA Ops:
  0.0 22.3 %copy-start = (f32[48,128,128]{2,1,0:T(8,128)S(1)}, f32[48,128,128]{2,1,0:T(8,128)}, u32[]{:S(2)}) copy-start(f32[48,128,128]{2,1,0:T(8,128)} %param.9) | copy-start | bytes 9437188
  0.0 8.7 %collective-permute-start = (f32[4,4,16,128]{3,2,1,0:T(8,128)}, f32[4,4,16,128]{3,2,1,0:T(8,128)S(1)}, u32[]{:S(2)}, u32[]{:S(2)}) collective-permute-start(f32[4,4,16,128]{3,2,1,0:T(8,128)} %param.7), channel_id=1, source_target_pairs={{0,8},{8,16},{16,24},{24,0},{1,9},{9,17},{17,25},{25,1},{2,10},{10... | collective-permute-start | bytes 393224 | tf_op jit(solution)/shard_map/ppermute | solution.py:13
  1.6 15.2 %collective-permute-start.2 = (f32[4,4,16,128]{3,2,1,0:T(8,128)}, f32[4,4,16,128]{3,2,1,0:T(8,128)S(1)}, u32[]{:S(2)}, u32[]{:S(2)}) collective-permute-start(f32[4,4,16,128]{3,2,1,0:T(8,128)} %param.7), channel_id=1, source_target_pairs={{0,24},{8,0},{16,8},{24,16},{1,25},{9,1},{17,9},{25,17},{2,26},{10... | collective-permute-start | bytes 393224 | tf_op jit(solution)/shard_map/ppermute | solution.py:15
  8.7 7.2 %collective-permute-start.1 = (f32[4,4,16,128]{3,2,1,0:T(8,128)S(1)}, f32[4,4,16,128]{3,2,1,0:T(8,128)S(1)}, u32[]{:S(2)}, u32[]{:S(2)}) collective-permute-start(f32[4,4,16,128]{3,2,1,0:T(8,128)S(1)} %collective-permute-done), channel_id=1, source_target_pairs={{0,8},{8,16},{16,24},{24,0},{1,9},{9,17},{17,25},{25,1},{2,10},{10... | collective-permute-start | bytes 393224 | tf_op jit(solution)/shard_map/ppermute | solution.py:13
  16.9 11.4 %copy-start.6 = (s32[48]{0:T(128)S(1)}, s32[48]{0:T(128)}, u32[]{:S(2)}) copy-start(s32[48]{0:T(128)} %get-tuple-element.21) | copy-start | bytes 580
  16.9 11.4 %copy-start.7 = (f32[48]{0:T(128)S(1)}, f32[48]{0:T(128)}, u32[]{:S(2)}) copy-start(f32[48]{0:T(128)} %compare_convert_fusion) | copy-start | bytes 580
  17.9 1.0 copy-start.2
  18.8 35.3 %copy-start.5 = (f32[1,4,16,128]{3,2,1,0:T(8,128)S(1)}, f32[1,4,16,128]{3,2,1,0:T(8,128)}, u32[]{:S(2)}) copy-start(f32[1,4,16,128]{3,2,1,0:T(8,128)} %get-tuple-element.20) | copy-start | bytes 98308
  18.8 35.4 %copy-start.1 = (f32[4,128,128]{2,1,0:T(8,128)S(1)}, f32[4,128,128]{2,1,0:T(8,128)}, u32[]{:S(2)}) copy-start(f32[4,128,128]{2,1,0:T(8,128)} %param.12) | copy-start | bytes 786436
  52.2 16.9 %collective-permute-start.3 = (f32[16,16,128]{2,1,0:T(8,128)S(1)}, f32[16,16,128]{2,1,0:T(8,128)S(1)}, u32[]{:S(2)}, u32[]{:S(2)}) collective-permute-start(f32[16,16,128]{2,1,0:T(8,128)S(1)} %dynamic-slice_bitcast_fusion.2), channel_id=1, source_target_pairs={{0,1},{1,2},{2,3},{3,4},{4,5},{5,6},{6,7},{8,9},{9,10},{10,11},{11... | collective-permute-start | bytes 393224 | tf_op jit(solution)/shard_map/ppermute | solution.py:23
  54.2 50.5 %copy-start.4 = (f32[1,4,16,128]{3,2,1,0:T(8,128)S(1)}, f32[1,4,16,128]{3,2,1,0:T(8,128)}, u32[]{:S(2)}) copy-start(f32[1,4,16,128]{3,2,1,0:T(8,128)} %get-tuple-element.19) | copy-start | bytes 98308
  78.3 49.7 %copy-start.8 = (f32[48]{0:T(128)S(1)}, f32[48]{0:T(128)}, u32[]{:S(2)}) copy-start(f32[48]{0:T(128)} %compare_convert_fusion) | copy-start | bytes 580
  102.8 16.0 %collective-permute-start.4 = (f32[16,16,128]{2,1,0:T(8,128)S(1)}, f32[16,16,128]{2,1,0:T(8,128)S(1)}, u32[]{:S(2)}, u32[]{:S(2)}) collective-permute-start(f32[16,16,128]{2,1,0:T(8,128)S(1)} %dynamic-slice_bitcast_fusion.1), channel_id=1, source_target_pairs={{0,1},{1,2},{2,3},{3,4},{4,5},{5,6},{6,7},{8,9},{9,10},{10,11},{11... | collective-permute-start | bytes 393224 | tf_op jit(solution)/shard_map/ppermute | solution.py:23
  104.8 50.1 %copy-start.3 = (f32[1,4,16,128]{3,2,1,0:T(8,128)S(1)}, f32[1,4,16,128]{3,2,1,0:T(8,128)}, u32[]{:S(2)}) copy-start(f32[1,4,16,128]{3,2,1,0:T(8,128)} %get-tuple-element.18) | copy-start | bytes 98308
  152.9 15.8 %collective-permute-start.5 = (f32[16,16,128]{2,1,0:T(8,128)S(1)}, f32[16,16,128]{2,1,0:T(8,128)S(1)}, u32[]{:S(2)}, u32[]{:S(2)}) collective-permute-start(f32[16,16,128]{2,1,0:T(8,128)S(1)} %dynamic-slice_bitcast_fusion), channel_id=1, source_target_pairs={{0,1},{1,2},{2,3},{3,4},{4,5},{5,6},{6,7},{8,9},{9,10},{10,11},{11... | collective-permute-start | bytes 393224 | tf_op jit(solution)/shard_map/ppermute | solution.py:23
